TPU v7x, 32 devices: a whole 2x2x4 slice. The times are simulated.
32 devices in a mesh: band: 4 (over y, core), grid: 8 (over z, x).
Axes of the slice: x: 2, y: 2, z: 4, core: 2. Of those that a mesh axis runs over, the one named last changes fastest.
Arguments:
- orbitals: float32 [64, 16, 4096], P('band', 'grid'), may hold values from -6 to 6
- potential: float32 [16, 4096], P('grid'), may hold values from 0 to 2
Outputs:
- rotated: bfloat16 [64, 16, 4096], P('band', 'grid')
All inputs are finite; a program needn't handle non-finite values. Where the computation divides by a largest or mean magnitude, that divisor is 1e-20 or more.
Results may differ from a plain program's by a relative error of at most 0.001.
The roundings to bfloat16 on the way count: a program that leaves them out, or rounds other values in their place, can miss the bound.
Values may be sent and summed in bfloat16 or wider, within the bound.
A program may use at most 64 MiB of HBM per device.

v0:
```python
import jax
import jax.numpy as jnp
from jax import lax
from jax.sharding import PartitionSpec as P

NX = 64
DEGREE = 2
NS_ITERS = 2


def with_halo(block, sides, width):
    for axis, dim in sides:
        count = lax.axis_size(axis)
        forward = [(i, i + 1) for i in range(count - 1)]
        forward.append((count - 1, 0))
        backward = [(target, source) for source, target in forward]
        low = lax.ppermute(
            lax.slice_in_dim(block, block.shape[dim] - width, None, axis=dim), axis, forward
        )
        high = lax.ppermute(lax.slice_in_dim(block, 0, width, axis=dim), axis, backward)
        block = jnp.concatenate([low, block, high], axis=dim)
    return block


def apply_inner(extended, potential):
    inner = extended[:, 1:-1]
    count = inner.shape[0]
    planes = inner.shape[1]
    square = inner.reshape(count, planes, NX, NX)
    sideways = jnp.roll(square, 1, 2) + jnp.roll(square, -1, 2)
    sideways = sideways + jnp.roll(square, 1, 3) + jnp.roll(square, -1, 3)
    beside = extended[:, 2:] + extended[:, :-2] + sideways.reshape(inner.shape)
    return 0.5 * (6.0 * inner - beside) + potential[None] * inner


def local(orbitals, potential):
    previous = orbitals
    current = orbitals
    for degree_step in range(DEGREE):
        extended = with_halo(current, (("grid", 1),), 1)
        applied = apply_inner(extended, potential)
        if degree_step == 0:
            following = (applied - 5.0 * current) / 3.0
        else:
            following = 2.0 * (applied - 5.0 * current) / 3.0 - previous
        previous = current
        current = following
    count, zplanes, width = orbitals.shape
    filtered = current.astype(jnp.bfloat16).reshape(count, zplanes * width)
    pieces = lax.all_to_all(filtered, "band", split_axis=1, concat_axis=0, tiled=True)
    total_cells = pieces.shape[1] * lax.axis_size("band") * lax.axis_size("grid")
    partial_value = (
        lax.dot_general(
            pieces, pieces, (((1,), (1,)), ((), ())), preferred_element_type=jnp.float32
        )
        / total_cells
    )
    gram = lax.psum(partial_value, ("band", "grid"))
    scale = jnp.max(jnp.sum(jnp.abs(gram), axis=1))
    identity_mat = jnp.eye(gram.shape[0], dtype=jnp.float32)
    upper = gram / scale
    lower = identity_mat
    for sweep in range(NS_ITERS):
        factor = 1.5 * identity_mat - 0.5 * jnp.dot(lower, upper, precision=lax.Precision.HIGHEST)
        upper = jnp.dot(upper, factor, precision=lax.Precision.HIGHEST)
        lower = jnp.dot(factor, lower, precision=lax.Precision.HIGHEST)
    root = (lower / jnp.sqrt(scale)).astype(jnp.bfloat16)
    turned = lax.dot_general(
        root, pieces, (((0,), (0,)), ((), ())), preferred_element_type=jnp.float32
    )
    turned = turned.astype(jnp.bfloat16)
    returned = lax.all_to_all(turned, "band", split_axis=0, concat_axis=1, tiled=True)
    return returned.reshape(count, zplanes, width)


def solution(mesh):
    placed = (P("band", "grid", None), P("grid", None))
    return jax.shard_map(
        local, mesh=mesh, in_specs=placed, out_specs=P("band", "grid", None), check_vma=False
    )
```

profile of v0, /device:TPU:0, one launch (start us, length us, event | category | flops | bytes accessed | tf_op | source)
XLA Modules:
  0.0 102.4 jit_solution(3121627851999156750)
XLA Ops:
  0.0 0.0 copy-start
  0.0 1.9 %fusion.24 = (f32[16,1,4096]{2,1,0:T(1,128)S(1)}, f32[16,1,4096]{2,1,0:T(1,128)S(1)}) fusion(f32[16,2,4096]{2,1,0:T(2,128)} %param.2), kind=kLoop, calls=%fused_computation.42 | loop fusion | bytes 1048576 | tf_op jit(solution)/shard_map/slice | solution.py:20
  1.9 6.1 %collective-permute-start = (f32[16,1,4096]{2,1,0:T(1,128)S(1)}, f32[16,1,4096]{2,1,0:T(1,128)S(1)}, u32[]{:S(2)}, u32[]{:S(2)}) collective-permute-start(f32[16,1,4096]{2,1,0:T(1,128)S(1)} %get-tuple-element.25), channel_id=1, source_target_pairs={{1,0},{2,1},{3,2},{4,3},{5,4},{6,5},{7,6},{0,7},{9,8},{10,9},{11,1... | collective-permute-start | bytes 786440 | tf_op jit(solution)/shard_map/ppermute | solution.py:20
  7.9 0.0 collective-permute-start.1
  7.9 0.0 copy-done
  7.9 0.6 reshape.35
  8.6 0.4 fusion.19
  8.9 0.4 fusion.20
  9.3 0.0 copy-start.1
  9.3 0.2 fusion.21
  9.5 0.5 copy-done.1
  10.1 0.9 fusion.4
  11.0 0.5 add.58
  11.5 2.0 %collective-permute-done = f32[16,1,4096]{2,1,0:T(1,128)S(1)} collective-permute-done((f32[16,1,4096]{2,1,0:T(1,128)S(1)}, f32[16,1,4096]{2,1,0:T(1,128)S(1)}, u32[]{:S(2)}, u32[]{:S(2)}) %collective-permute-start) | collective-permute-done | bytes 262176 | tf_op jit(solution)/shard_map/ppermute | solution.py:20
  13.5 5.0 %collective-permute-done.1 = f32[16,1,4096]{2,1,0:T(1,128)} collective-permute-done((f32[16,1,4096]{2,1,0:T(1,128)S(1)}, f32[16,1,4096]{2,1,0:T(1,128)}, u32[]{:S(2)}, u32[]{:S(2)}) %collective-permute-start.1) | collective-permute-done | bytes 262176 | tf_op jit(solution)/shard_map/ppermute | solution.py:17
  18.5 2.4 %broadcast_multiply_fusion = (f32[16,2,4096]{2,1,0:T(2,128)S(1)}, f32[16,2,4096]{2,1,0:T(2,128)S(1)}) fusion(f32[16,2,4096]{2,1,0:T(2,128)S(1)} %copy-done, f32[2,4096]{1,0:T(2,128)S(1)} %copy-done.1, f32[16,2,4096]{2,1,0:T(2,128)S(1)} %add.58, f32[16,1,4096]{2,1,0:T(1,128)} %collective-permute-done.1, f32[16,1,4096]{2,1,0:T(1,128)S(1)} %collective-permute-done), kind=kLoop, calls=%fused_computation.26 | loop fusion | flops 1572864 | bytes 2654208 | tf_op jit(solution)/shard_map/div | solution.py:43
  21.0 0.6 reshape.36
  21.6 0.4 fusion.16
  22.0 0.2 fusion.17
  22.2 0.4 fusion.15
  22.5 1.3 %fusion.23 = (f32[16,1,4096]{2,1,0:T(1,128)}, f32[16,1,4096]{2,1,0:T(1,128)}) fusion(f32[16,2,4096]{2,1,0:T(2,128)S(1)} %get-tuple-element.5), kind=kLoop, calls=%fused_computation.41 | loop fusion | bytes 1048576 | tf_op jit(solution)/shard_map/slice | solution.py:20
  23.9 3.5 %collective-permute-start.2 = (f32[16,1,4096]{2,1,0:T(1,128)}, f32[16,1,4096]{2,1,0:T(1,128)S(1)}, u32[]{:S(2)}, u32[]{:S(2)}) collective-permute-start(f32[16,1,4096]{2,1,0:T(1,128)} %get-tuple-element.23), channel_id=1, source_target_pairs={{1,0},{2,1},{3,2},{4,3},{5,4},{6,5},{7,6},{0,7},{9,8},{10,9},{11,1... | collective-permute-start | bytes 786440 | tf_op jit(solution)/shard_map/ppermute | solution.py:20
  27.3 0.0 collective-permute-start.3
  27.4 0.9 fusion.6
  28.2 0.5 add.65
  28.8 8.5 %collective-permute-done.2 = f32[16,1,4096]{2,1,0:T(1,128)S(1)} collective-permute-done((f32[16,1,4096]{2,1,0:T(1,128)}, f32[16,1,4096]{2,1,0:T(1,128)S(1)}, u32[]{:S(2)}, u32[]{:S(2)}) %collective-permute-start.2) | collective-permute-done | bytes 262176 | tf_op jit(solution)/shard_map/ppermute | solution.py:20
  37.2 0.3 collective-permute-done.3
  37.5 2.6 %subtract_convert_fusion = bf16[16,2,4096]{2,1,0:T(2,128)(2,1)S(1)} fusion(f32[16,2,4096]{2,1,0:T(2,128)S(1)} %copy-done, f32[16,2,4096]{2,1,0:T(2,128)S(1)} %get-tuple-element.6, f32[16,2,4096]{2,1,0:T(2,128)S(1)} %add.65, f32[16,2,4096]{2,1,0:T(2,128)S(1)} %get-tuple-element.5, f32[16,1,4096]{2,1,0:T(1,128)} %collective-permute-done.3, ...), kind=kLoop, calls=%fused_computation.24 | loop fusion | flops 1835008 | bytes 2916352 | tf_op jit(solution)/shard_map/convert_element_type | solution.py:49
  40.1 0.1 all_to_all.26
  40.2 0.2 copy.7
  40.3 8.6 %all_to_all.35 = bf16[16,4,2048]{2,0,1:T(8,128)(2,1)S(1)} all-to-all(bf16[16,4,2048]{2,0,1:T(8,128)(2,1)S(1)} %copy.7), channel_id=1, replica_groups=mesh['band'=4,'grid'=8] {'band'}, dimensions={1} | all-to-all | bytes 524288 | tf_op jit(solution)/shard_map/all_to_all | solution.py:50
  48.9 0.2 convolution_multiply_fusion.2
  49.1 39.0 %psum.7 = f32[64,64]{1,0:T(8,128)S(1)} all-reduce(f32[64,64]{1,0:T(8,128)S(1)} %convolution_multiply_fusion.2), channel_id=1, replica_groups=mesh['band'=4,'grid'=8] {'band','grid'}, use_global_device_ids=true, to_apply=%region_0.1 | all-reduce | flops 4096 | bytes 32768 | tf_op jit(solution)/shard_map/psum | solution.py:58
  88.1 0.1 abs_reduce_fusion
  88.2 0.6 reduce_max.9
  88.8 0.8 fusion.1
  89.6 0.8 fusion.14
  90.4 0.1 fusion.13
  91.3 0.2 fusion
  91.5 0.2 fusion.2
  91.6 0.2 convolution_convert_fusion
  91.9 9.4 %all_to_all.36 = bf16[4,16,2048]{2,1,0:T(8,128)(2,1)S(1)} all-to-all(bf16[4,16,2048]{2,1,0:T(8,128)(2,1)S(1)} %bitcast.21), channel_id=1, replica_groups=mesh['band'=4,'grid'=8] {'band'}, dimensions={0} | all-to-all | bytes 524288 | tf_op jit(solution)/shard_map/all_to_all | solution.py:72
  101.2 0.2 copy.8
  101.5 0.9 reshape.37
  (3 shorter events, 0.1 us)
Async XLA Ops:
  0.0 7.9 %copy-start = (f32[16,2,4096]{2,1,0:T(2,128)S(1)}, f32[16,2,4096]{2,1,0:T(2,128)}, u32[]{:S(2)}) copy-start(f32[16,2,4096]{2,1,0:T(2,128)} %param.2) | copy-start | bytes 1572868
  1.9 11.6 %collective-permute-start = (f32[16,1,4096]{2,1,0:T(1,128)S(1)}, f32[16,1,4096]{2,1,0:T(1,128)S(1)}, u32[]{:S(2)}, u32[]{:S(2)}) collective-permute-start(f32[16,1,4096]{2,1,0:T(1,128)S(1)} %get-tuple-element.25), channel_id=1, source_target_pairs={{1,0},{2,1},{3,2},{4,3},{5,4},{6,5},{7,6},{0,7},{9,8},{10,9},{11,1... | collective-permute-start | bytes 786440 | tf_op jit(solution)/shard_map/ppermute | solution.py:20
  7.9 10.6 %collective-permute-start.1 = (f32[16,1,4096]{2,1,0:T(1,128)S(1)}, f32[16,1,4096]{2,1,0:T(1,128)}, u32[]{:S(2)}, u32[]{:S(2)}) collective-permute-start(f32[16,1,4096]{2,1,0:T(1,128)S(1)} %get-tuple-element.26), channel_id=1, source_target_pairs={{0,1},{1,2},{2,3},{3,4},{4,5},{5,6},{6,7},{7,0},{8,9},{9,10},{10,1... | collective-permute-start | bytes 786440 | tf_op jit(solution)/shard_map/ppermute | solution.py:17
  9.3 0.8 copy-start.1
  23.9 13.4 %collective-permute-start.2 = (f32[16,1,4096]{2,1,0:T(1,128)}, f32[16,1,4096]{2,1,0:T(1,128)S(1)}, u32[]{:S(2)}, u32[]{:S(2)}) collective-permute-start(f32[16,1,4096]{2,1,0:T(1,128)} %get-tuple-element.23), channel_id=1, source_target_pairs={{1,0},{2,1},{3,2},{4,3},{5,4},{6,5},{7,6},{0,7},{9,8},{10,9},{11,1... | collective-permute-start | bytes 786440 | tf_op jit(solution)/shard_map/ppermute | solution.py:20
  27.3 10.2 %collective-permute-start.3 = (f32[16,1,4096]{2,1,0:T(1,128)}, f32[16,1,4096]{2,1,0:T(1,128)}, u32[]{:S(2)}, u32[]{:S(2)}) collective-permute-start(f32[16,1,4096]{2,1,0:T(1,128)} %get-tuple-element.24), channel_id=1, source_target_pairs={{0,1},{1,2},{2,3},{3,4},{4,5},{5,6},{6,7},{7,0},{8,9},{9,10},{10,1... | collective-permute-start | bytes 786440 | tf_op jit(solution)/shard_map/ppermute | solution.py:17
where the time goes:
time: 103 us; the launch traced here: 102 us
  blocking collectives  56.9 us (55%)
  waiting for transfers between devices  15.7 us (15%)
  starting transfers between devices  9.52 us (9%)
  local copies, waits for them, and re-layouts  9.32 us (9%)
  other arithmetic  7.48 us (7%)
  matrix products  2.54 us (2%)
    psum x1, blocking collectives, local(): gram = lax.psum(partial_value, ('band', 'grid'))  39 us
    ppermute x2, waiting for transfers between devices, with_halo(): lax.ppermute(lax.slice_in_dim(block, 0, width, axis=dim), axis, backward)  10.5 us
    ppermute x2, starting transfers between devices, with_halo(): lax.ppermute(lax.slice_in_dim(block, 0, width, axis=dim), axis, backward)  9.51 us
    all_to_all x1, blocking collectives, local(): lax.all_to_all(turned, 'band', split_axis=0, concat_axis=1, tiled=True)  9.36 us
    all_to_all x1, blocking collectives, local(): lax.all_to_all(filtered, 'band', split_axis=1, concat_axis=0, tiled=True)  8.59 us
    ppermute x2, waiting for transfers between devices, with_halo(): lax.ppermute(lax.slice_in_dim(block, block.shape[dim] - width, None, axis...  5.27 us
    slice x2, local copies, waits for them, and re-layouts, with_halo(): lax.slice_in_dim(block, 0, width, axis=dim)  3.21 us
    convert_element_type x1, other arithmetic, local(): filtered = current.astype(jnp.bfloat16).reshape(count, zplanes * width)  2.58 us
  transfers between devices with their start and end apart: 4, of which 4 were waited for; matrix products, arithmetic and copies ran while one was open for 4% of the time, Pallas kernels for 0%

commit v1 on v0

--- a/solution.py
+++ b/solution.py
@@ -1,11 +1,21 @@
+import functools
 import jax
 import jax.numpy as jnp
 from jax import lax
 from jax.sharding import PartitionSpec as P
+from jax.lax import all_gather
 
 NX = 64
 DEGREE = 2
 NS_ITERS = 2
+
+
+def column_review(payload, mesh_ax):
+    y_new = jnp.sum(all_gather(payload, mesh_ax), axis=0)
+    return y_new
+
+
+start_links = functools.partial(column_review, mesh_ax=("band", "grid"))
 
 
 def with_halo(block, sides, width):
@@ -55,7 +65,7 @@
         )
         / total_cells
     )
-    gram = lax.psum(partial_value, ("band", "grid"))
+    gram = start_links(partial_value)
     scale = jnp.max(jnp.sum(jnp.abs(gram), axis=1))
     identity_mat = jnp.eye(gram.shape[0], dtype=jnp.float32)
     upper = gram / scale

time: 103 us -> 135 us (1.31)
  blocking collectives: 56.9 us -> 89.2 us
    all_gather x0 -> x1, blocking collectives: none -> 72.2 us  [column_review(): y_new = jnp.sum(all_gather(payload, mesh_ax), axis=0)]
    psum x1 -> x0, blocking collectives: 39 us -> none  [local(): gram = lax.psum(partial_value, ('band', 'grid'))]
  transfers between devices with their start and end apart: 4 -> 4, of which waited for: 4 -> 4; matrix products, arithmetic and copies ran while one was open for 4% -> 3% of each run, Pallas kernels for 0% -> 0%
where the time goes in v1:
time: 135 us
  blocking collectives  89.2 us (66%)
  waiting for transfers between devices  15.7 us (12%)
  starting transfers between devices  9.52 us (7%)
  local copies, waits for them, and re-layouts  9.32 us (7%)
  other arithmetic  7.57 us (6%)
  matrix products  2.54 us (2%)
    all_gather x1, blocking collectives, column_review(): y_new = jnp.sum(all_gather(payload, mesh_ax), axis=0)  72.2 us
    ppermute x2, waiting for transfers between devices, with_halo(): lax.ppermute(lax.slice_in_dim(block, 0, width, axis=dim), axis, backward)  10.5 us
    ppermute x2, starting transfers between devices, with_halo(): lax.ppermute(lax.slice_in_dim(block, 0, width, axis=dim), axis, backward)  9.51 us
    all_to_all x1, blocking collectives, local(): lax.all_to_all(filtered, 'band', split_axis=1, concat_axis=0, tiled=True)  8.59 us
    all_to_all x1, blocking collectives, local(): lax.all_to_all(turned, 'band', split_axis=0, concat_axis=1, tiled=True)  8.39 us
    ppermute x2, waiting for transfers between devices, with_halo(): lax.ppermute(lax.slice_in_dim(block, block.shape[dim] - width, None, axis...  5.27 us
    slice x2, local copies, waits for them, and re-layouts, with_halo(): lax.slice_in_dim(block, 0, width, axis=dim)  3.21 us
  transfers between devices with their start and end apart: 4, of which 4 were waited for; matrix products, arithmetic and copies ran while one was open for 3% of the time, Pallas kernels for 0%

profile of v1, /device:TPU:0, one launch (start us, length us, event | category | flops | bytes accessed | tf_op | source)
XLA Modules:
  0.0 134.7 jit_solution(11696370182459699822)
XLA Ops:
  0.0 0.0 copy-start
  0.0 1.9 %fusion.24 = (f32[16,1,4096]{2,1,0:T(1,128)S(1)}, f32[16,1,4096]{2,1,0:T(1,128)S(1)}) fusion(f32[16,2,4096]{2,1,0:T(2,128)} %param.2), kind=kLoop, calls=%fused_computation.42 | loop fusion | bytes 1048576 | tf_op jit(solution)/shard_map/slice | solution.py:30
  1.9 6.1 %collective-permute-start = (f32[16,1,4096]{2,1,0:T(1,128)S(1)}, f32[16,1,4096]{2,1,0:T(1,128)S(1)}, u32[]{:S(2)}, u32[]{:S(2)}) collective-permute-start(f32[16,1,4096]{2,1,0:T(1,128)S(1)} %get-tuple-element.25), channel_id=1, source_target_pairs={{1,0},{2,1},{3,2},{4,3},{5,4},{6,5},{7,6},{0,7},{9,8},{10,9},{11,1... | collective-permute-start | bytes 786440 | tf_op jit(solution)/shard_map/ppermute | solution.py:30
  7.9 0.0 collective-permute-start.1
  7.9 0.0 copy-done
  7.9 0.6 reshape.35
  8.6 0.4 fusion.19
  8.9 0.4 fusion.20
  9.3 0.0 copy-start.1
  9.3 0.2 fusion.21
  9.5 0.5 copy-done.1
  10.1 0.9 fusion.4
  11.0 0.5 add.56
  11.5 2.0 %collective-permute-done = f32[16,1,4096]{2,1,0:T(1,128)S(1)} collective-permute-done((f32[16,1,4096]{2,1,0:T(1,128)S(1)}, f32[16,1,4096]{2,1,0:T(1,128)S(1)}, u32[]{:S(2)}, u32[]{:S(2)}) %collective-permute-start) | collective-permute-done | bytes 262176 | tf_op jit(solution)/shard_map/ppermute | solution.py:30
  13.5 5.0 %collective-permute-done.1 = f32[16,1,4096]{2,1,0:T(1,128)} collective-permute-done((f32[16,1,4096]{2,1,0:T(1,128)S(1)}, f32[16,1,4096]{2,1,0:T(1,128)}, u32[]{:S(2)}, u32[]{:S(2)}) %collective-permute-start.1) | collective-permute-done | bytes 262176 | tf_op jit(solution)/shard_map/ppermute | solution.py:27
  18.5 2.4 %broadcast_multiply_fusion = (f32[16,2,4096]{2,1,0:T(2,128)S(1)}, f32[16,2,4096]{2,1,0:T(2,128)S(1)}) fusion(f32[16,2,4096]{2,1,0:T(2,128)S(1)} %copy-done, f32[2,4096]{1,0:T(2,128)S(1)} %copy-done.1, f32[16,2,4096]{2,1,0:T(2,128)S(1)} %add.56, f32[16,1,4096]{2,1,0:T(1,128)} %collective-permute-done.1, f32[16,1,4096]{2,1,0:T(1,128)S(1)} %collective-permute-done), kind=kLoop, calls=%fused_computation.26 | loop fusion | flops 1572864 | bytes 2654208 | tf_op jit(solution)/shard_map/div | solution.py:53
  21.0 0.6 reshape.36
  21.6 0.4 fusion.16
  22.0 0.2 fusion.17
  22.2 0.4 fusion.15
  22.5 1.3 fusion.23
  23.9 3.5 %collective-permute-start.2 = (f32[16,1,4096]{2,1,0:T(1,128)}, f32[16,1,4096]{2,1,0:T(1,128)S(1)}, u32[]{:S(2)}, u32[]{:S(2)}) collective-permute-start(f32[16,1,4096]{2,1,0:T(1,128)} %get-tuple-element.23), channel_id=1, source_target_pairs={{1,0},{2,1},{3,2},{4,3},{5,4},{6,5},{7,6},{0,7},{9,8},{10,9},{11,1... | collective-permute-start | bytes 786440 | tf_op jit(solution)/shard_map/ppermute | solution.py:30
  27.3 0.0 collective-permute-start.3
  27.4 0.9 fusion.6
  28.2 0.5 add.63
  28.8 8.5 %collective-permute-done.2 = f32[16,1,4096]{2,1,0:T(1,128)S(1)} collective-permute-done((f32[16,1,4096]{2,1,0:T(1,128)}, f32[16,1,4096]{2,1,0:T(1,128)S(1)}, u32[]{:S(2)}, u32[]{:S(2)}) %collective-permute-start.2) | collective-permute-done | bytes 262176 | tf_op jit(solution)/shard_map/ppermute | solution.py:30
  37.2 0.3 collective-permute-done.3
  37.5 2.6 %subtract_convert_fusion = bf16[16,2,4096]{2,1,0:T(2,128)(2,1)S(1)} fusion(f32[16,2,4096]{2,1,0:T(2,128)S(1)} %copy-done, f32[16,2,4096]{2,1,0:T(2,128)S(1)} %get-tuple-element.6, f32[16,2,4096]{2,1,0:T(2,128)S(1)} %add.63, f32[16,2,4096]{2,1,0:T(2,128)S(1)} %get-tuple-element.5, f32[16,1,4096]{2,1,0:T(1,128)} %collective-permute-done.3, ...), kind=kLoop, calls=%fused_computation.24 | loop fusion | flops 1835008 | bytes 2916352 | tf_op jit(solution)/shard_map/convert_element_type | solution.py:59
  40.1 0.1 all_to_all.26
  40.2 0.2 copy.9
  40.3 8.6 %all_to_all.35 = bf16[16,4,2048]{2,0,1:T(8,128)(2,1)S(1)} all-to-all(bf16[16,4,2048]{2,0,1:T(8,128)(2,1)S(1)} %copy.9), channel_id=1, replica_groups=mesh['band'=4,'grid'=8] {'band'}, dimensions={1} | all-to-all | bytes 524288 | tf_op jit(solution)/shard_map/all_to_all | solution.py:60
  48.9 0.2 convolution_multiply_fusion.2
  49.1 72.2 %all-gather = f32[2048,64]{1,0:T(8,128)S(1)} all-gather(f32[64,64]{1,0:T(8,128)S(1)} %convolution_multiply_fusion.2), channel_id=2, replica_groups=mesh['band'=4,'grid'=8] {'band','grid'}, dimensions={0}, use_global_device_ids=true | all-gather | bytes 540672 | tf_op jit(solution)/shard_map/all_gather | solution.py:14
  121.3 0.1 reduce_sum.18
  121.4 0.1 abs_reduce_fusion
  121.5 0.6 reduce_max.9
  122.2 0.8 fusion.1
  123.0 0.8 fusion.14
  123.8 0.1 fusion.13
  124.6 0.2 fusion
  124.8 0.2 fusion.2
  125.0 0.2 convolution_convert_fusion
  125.2 8.4 %all_to_all.36 = bf16[4,16,2048]{2,1,0:T(8,128)(2,1)S(1)} all-to-all(bf16[4,16,2048]{2,1,0:T(8,128)(2,1)S(1)} %bitcast.23), channel_id=1, replica_groups=mesh['band'=4,'grid'=8] {'band'}, dimensions={0} | all-to-all | bytes 524288 | tf_op jit(solution)/shard_map/all_to_all | solution.py:82
  133.6 0.2 copy.10
  133.8 0.9 reshape.37
  (3 shorter events, 0.1 us)
Async XLA Ops:
  0.0 7.9 %copy-start = (f32[16,2,4096]{2,1,0:T(2,128)S(1)}, f32[16,2,4096]{2,1,0:T(2,128)}, u32[]{:S(2)}) copy-start(f32[16,2,4096]{2,1,0:T(2,128)} %param.2) | copy-start | bytes 1572868
  1.9 11.6 %collective-permute-start = (f32[16,1,4096]{2,1,0:T(1,128)S(1)}, f32[16,1,4096]{2,1,0:T(1,128)S(1)}, u32[]{:S(2)}, u32[]{:S(2)}) collective-permute-start(f32[16,1,4096]{2,1,0:T(1,128)S(1)} %get-tuple-element.25), channel_id=1, source_target_pairs={{1,0},{2,1},{3,2},{4,3},{5,4},{6,5},{7,6},{0,7},{9,8},{10,9},{11,1... | collective-permute-start | bytes 786440 | tf_op jit(solution)/shard_map/ppermute | solution.py:30
  7.9 10.6 %collective-permute-start.1 = (f32[16,1,4096]{2,1,0:T(1,128)S(1)}, f32[16,1,4096]{2,1,0:T(1,128)}, u32[]{:S(2)}, u32[]{:S(2)}) collective-permute-start(f32[16,1,4096]{2,1,0:T(1,128)S(1)} %get-tuple-element.26), channel_id=1, source_target_pairs={{0,1},{1,2},{2,3},{3,4},{4,5},{5,6},{6,7},{7,0},{8,9},{9,10},{10,1... | collective-permute-start | bytes 786440 | tf_op jit(solution)/shard_map/ppermute | solution.py:27
  9.3 0.8 copy-start.1
  23.9 13.4 %collective-permute-start.2 = (f32[16,1,4096]{2,1,0:T(1,128)}, f32[16,1,4096]{2,1,0:T(1,128)S(1)}, u32[]{:S(2)}, u32[]{:S(2)}) collective-permute-start(f32[16,1,4096]{2,1,0:T(1,128)} %get-tuple-element.23), channel_id=1, source_target_pairs={{1,0},{2,1},{3,2},{4,3},{5,4},{6,5},{7,6},{0,7},{9,8},{10,9},{11,1... | collective-permute-start | bytes 786440 | tf_op jit(solution)/shard_map/ppermute | solution.py:30
  27.3 10.2 %collective-permute-start.3 = (f32[16,1,4096]{2,1,0:T(1,128)}, f32[16,1,4096]{2,1,0:T(1,128)}, u32[]{:S(2)}, u32[]{:S(2)}) collective-permute-start(f32[16,1,4096]{2,1,0:T(1,128)} %get-tuple-element.24), channel_id=1, source_target_pairs={{0,1},{1,2},{2,3},{3,4},{4,5},{5,6},{6,7},{7,0},{8,9},{9,10},{10,1... | collective-permute-start | bytes 786440 | tf_op jit(solution)/shard_map/ppermute | solution.py:27
